TPU v7x, 32 devices: a whole 2x2x4 slice. The times are simulated.
32 devices in a mesh: tok: 8 (over z, y), exp: 4 (over x, core).
Axes of the slice: x: 2, y: 2, z: 4, core: 2. Of those that a mesh axis runs over, the one named last changes fastest.
Arguments:
- tokens: bfloat16 [12, 8192, 1024], P(None, 'tok'), may hold values from -24 to 24
- slot_params: bfloat16 [1024, 128], P(None, 'exp'), may hold values from -2 to 2
- w_in: bfloat16 [64, 1024, 4096], P('exp', None, 'tok'), may hold values from -0.75 to 0.75
- w_out: bfloat16 [64, 4096, 1024], P('exp', 'tok'), may hold values from -0.1875 to 0.1875
Outputs:
- mixed: bfloat16 [12, 8192, 1024], P(None, 'tok', 'exp')
All inputs are finite; a program needn't handle non-finite values.
Results may differ from a plain program's by a relative error of at most 0.0072.
Values may be sent and summed in bfloat16 or wider, within the bound.
A program may use at most 192 MiB of HBM per device.

v0:
```python
import jax
import jax.numpy as jnp
from jax import lax
from jax.sharding import PartitionSpec as P

SLOTS_PER = 2


def shards(tokens, slot_params, w_in, w_out):
    own_width = slot_params.shape[1]
    own_logits = jnp.einsum("std,dj->sjt", tokens, slot_params, preferred_element_type=jnp.float32)
    all_logits = lax.all_gather(own_logits, "exp", axis=1, tiled=True)
    local_max = jnp.max(own_logits, axis=2)
    slot_peak = lax.pmax(local_max, "tok")
    dexp = jnp.exp(own_logits - slot_peak[:, :, None])
    local_den = jnp.sum(dexp, axis=2)
    dweight = dexp.astype(jnp.bfloat16)
    local_sum = jnp.einsum("sjt,std->sjd", dweight, tokens, preferred_element_type=jnp.float32)
    slot_sum, slot_den = lax.psum((local_sum, local_den), "tok")
    slot_in = (slot_sum / slot_den[:, :, None]).astype(jnp.bfloat16)
    seq_count = tokens.shape[0]
    local_experts = w_in.shape[0]
    width = tokens.shape[2]
    grouped = slot_in.reshape(seq_count, local_experts, SLOTS_PER, width)
    hidden = jax.nn.gelu(
        jnp.einsum("sepd,edf->sepf", grouped, w_in, preferred_element_type=jnp.float32),
        approximate=True,
    ).astype(jnp.bfloat16)
    partial_out = jnp.einsum("sepf,efd->sepd", hidden, w_out, preferred_element_type=jnp.float32)
    partial_out = partial_out.reshape(seq_count, own_width, width)
    summed = lax.psum(partial_out, "tok").astype(jnp.bfloat16)
    slot_out = lax.all_to_all(summed, "exp", split_axis=2, concat_axis=1, tiled=True)
    comb_max = jnp.max(all_logits, axis=1)
    cexp = jnp.exp(all_logits - comb_max[:, None, :])
    cweight = (cexp / jnp.sum(cexp, axis=1)[:, None, :]).astype(jnp.bfloat16)
    mixed = jnp.einsum("sjt,sjd->std", cweight, slot_out, preferred_element_type=jnp.float32)
    return mixed.astype(jnp.bfloat16)


def solution(mesh):
    return jax.shard_map(
        shards,
        mesh=mesh,
        in_specs=(
            P(None, "tok", None),
            P(None, "exp"),
            P("exp", None, "tok"),
            P("exp", "tok", None),
        ),
        out_specs=P(None, "tok", "exp"),
        check_vma=False,
    )
```

profile of v0, /device:TPU:0, one launch (start us, length us, event | category | flops | bytes accessed | tf_op | source)
XLA Modules:
  0.0 546.4 jit_solution(2624365932778062341)
XLA Ops:
  7.4 0.0 copy-start
  7.4 0.0 all-reduce.3.cloned.1.call-start
  7.4 0.8 copy-done
  8.2 12.3 %fusion.28 = (f32[12,32]{1,0:T(8,128)S(1)}, f32[12,32,1024]{2,1,0:T(8,128)S(1)}) fusion(bf16[12,1024,1024]{2,1,0:T(8,128)(2,1)} %param.4, bf16[1024,32]{0,1:T(8,128)(2,1)S(1)} %copy-done), kind=kOutput, calls=%fused_computation.28 | convolution fusion | flops 805699200 | bytes 26805760 | tf_op jit(solution)/shard_map/std,dj->sjt/dot_general | solution.py:11
  20.5 0.0 copy-start.2
  20.5 23.4 %pmax.7 = f32[12,32]{1,0:T(8,128)S(1)} all-reduce(f32[12,32]{1,0:T(8,128)S(1)} %get-tuple-element.5), channel_id=1, replica_groups=mesh['tok'=8,'exp'=4] {'tok'}, use_global_device_ids=true, to_apply=%region_3.0 | all-reduce | flops 384 | bytes 3072 | tf_op jit(solution)/shard_map/pmax | solution.py:14
  43.9 11.7 %fusion.23 = f32[12,32,1024]{2,1,0:T(8,128)} fusion(bf16[12,1024,1024]{2,1,0:T(8,128)(2,1)} %param.4, f32[12,32,1024]{2,1,0:T(8,128)S(1)} %get-tuple-element.6, f32[12,32]{1,0:T(8,128)S(1)} %pmax.7), kind=kOutput, calls=%fused_computation.24 | convolution fusion | flops 806092800 | bytes 28313088 | tf_op jit(solution)/shard_map/sjt,std->sjd/dot_general | solution.py:18
  55.6 0.0 copy-done.2
  55.6 0.0 all-reduce.3.cloned.1.call-update
  55.6 0.0 all-gather.2.cloned.1.call-start
  55.6 0.5 all-gather.2.cloned.1.call-update
  56.2 1.8 fusion.6
  57.9 18.4 %psum.22 = f32[12,32]{1,0:T(8,128)S(1)} all-reduce(f32[12,32]{1,0:T(8,128)S(1)} %fusion.6), channel_id=1, replica_groups=mesh['tok'=8,'exp'=4] {'tok'}, use_global_device_ids=true, to_apply=%region_6.0 | all-reduce | flops 384 | bytes 3072 | tf_op jit(solution)/shard_map/psum | solution.py:19
  76.3 66.0 %all-reduce.3.cloned.1.call-done = f32[12,32,1024]{2,1,0:T(8,128)} async-done(((f32[12,32,1024]{2,1,0:T(8,128)}), f32[12,32,1024]{2,1,0:T(8,128)}) %all-reduce.3.cloned.1.call-update) | async-done | bytes 1572880 | tf_op jit(solution)/shard_map/psum | solution.py:19
  142.3 1.6 divide_convert_fusion.2
  144.0 0.4 copy.20
  144.4 8.7 %fusion.20 = bf16[12,16,2,512]{3,0,2,1:T(8,128)(2,1)S(1)} fusion(bf16[12,16,2,1024]{3,0,2,1:T(8,128)(2,1)S(1)} %bitcast.48, bf16[16,1024,512]{2,1,0:T(8,128)(2,1)} %param.6), kind=kOutput, calls=%fused_computation.23 | convolution fusion | flops 404422656 | bytes 17956864 | tf_op jit(solution)/shard_map/sepd,edf->sepf/dot_general | solution.py:26
  153.2 8.7 %fusion.1 = f32[16,12,2,1024]{3,1,2,0:T(8,128)S(1)} fusion(bf16[12,16,2,512]{3,0,2,1:T(8,128)(2,1)S(1)} %fusion.20, bf16[16,512,1024]{2,1,0:T(8,128)(2,1)} %param.7), kind=kOutput, calls=%fused_computation.1 | convolution fusion | flops 402653184 | bytes 18743296 | tf_op jit(solution)/shard_map/sepf,efd->sepd/dot_general | solution.py:29
  161.9 6.5 %copy.13 = f32[12,32,1024]{1,0,2:T(8,128)} copy(f32[12,32,1024]{2,0,1:T(8,128)S(1)} %bitcast.47) | data formatting | bytes 3145728 | tf_op jit(solution)/shard_map/reshape | solution.py:30
  168.4 326.7 %all-reduce.4 = bf16[12,32,1024]{1,0,2:T(8,128)(2,1)} all-reduce(f32[12,32,1024]{1,0,2:T(8,128)} %copy.13), channel_id=1, replica_groups=mesh['tok'=8,'exp'=4] {'tok'}, use_global_device_ids=true, to_apply=%region_7.0 | all-reduce | flops 393216 | bytes 2359296 | tf_op jit(solution)/shard_map/psum | solution.py:31
  495.1 5.0 reshape.15
  500.1 14.2 %all_to_all.18 = bf16[4,2,49152]{2,1,0:T(2,128)(2,1)S(1)} all-to-all(bf16[4,2,49152]{2,1,0:T(2,128)(2,1)S(1)} %reshape.15), channel_id=1, replica_groups=mesh['tok'=8,'exp'=4] {'exp'}, dimensions={0} | all-to-all | bytes 1572864 | tf_op jit(solution)/shard_map/all_to_all | solution.py:32
  514.3 4.1 reshape.16
  518.4 5.1 copy.21
  523.6 0.1 copy.15
  523.7 0.0 all-gather.2.cloned.1.call-done
  523.7 5.8 %fusion.29 = f32[12,1024]{1,0:T(8,128)S(1)} fusion(f32[12,128,1024]{2,1,0:T(8,128)} %all-gather.2.cloned.1.call-done), kind=kOutput, calls=%fused_computation.29 | output fusion | flops 3145855 | bytes 6340608 | tf_op jit(solution)/shard_map/sub | solution.py:34
  529.5 0.0 copy-start.1
  529.6 9.4 %convolution_convert_fusion = bf16[12,1024,256]{2,1,0:T(8,128)(2,1)} fusion(bf16[12,128,256]{2,1,0:T(8,128)(2,1)S(1)} %bitcast.50, f32[12,1024]{1,0:T(8,128)S(1)} %fusion.29, f32[12,128,1024]{2,1,0:T(8,128)} %all-gather.2.cloned.1.call-done), kind=kOutput, calls=%fused_computation.7 | convolution fusion | flops 813183104 | bytes 13418496 | tf_op jit(solution)/shard_map/sjt,sjd->std/dot_general | solution.py:36
  539.0 0.0 copy-done.1
Async XLA Ops:
  7.4 0.8 copy-start
  7.4 135.0 %all-reduce.3.cloned.1.call-start = ((), (), s32[]{:S(2)}) async-start(), calls=%async_computation.2 | async-start | bytes 3145728 | tf_op jit(solution)/shard_map/psum | solution.py:19
  20.5 35.0 %copy-start.2 = (f32[12,32,1024]{2,1,0:T(8,128)}, f32[12,32,1024]{2,1,0:T(8,128)S(1)}, u32[]{:S(2)}) copy-start(f32[12,32,1024]{2,1,0:T(8,128)S(1)} %get-tuple-element.6) | copy-start | bytes 4718596
  55.6 468.1 %all-gather.2.cloned.1.call-start = ((), (), s32[]{:S(2)}) async-start(), calls=%async_computation.1 | async-start | bytes 7864320 | tf_op jit(solution)/shard_map/all_gather | solution.py:12
  529.5 9.4 %copy-start.1 = (bf16[1024,32]{0,1:T(8,128)(2,1)S(1)}, bf16[1024,32]{0,1:T(8,128)(2,1)}, u32[]{:S(2)}) copy-start(bf16[1024,32]{0,1:T(8,128)(2,1)} %param.5) | copy-start | bytes 196612
Sparse Core Ops, SparseCore 0:
  55.7 86.5 all-reduce.2
Sparse Core Ops, SparseCore 1:
  57.6 43.5 all-gather.1
where the time goes:
time: 547 us; the launch traced here: 546 us
  blocking collectives  383 us (70%)
  waiting for transfers between devices  66.6 us (12%)
  matrix products  50.8 us (9%)
  local copies, waits for them, and re-layouts  22.2 us (4%)
  between operations  14.9 us (3%)
  other arithmetic  9.19 us (2%)
    psum x1, blocking collectives, shards(): summed = lax.psum(partial_out, 'tok').astype(jnp.bfloat16)  327 us
    psum x1, waiting for transfers between devices, shards(): slot_sum, slot_den = lax.psum((local_sum, local_den), 'tok')  66 us
    pmax x1, blocking collectives, shards(): slot_peak = lax.pmax(local_max, 'tok')  23.4 us
    psum x1, blocking collectives, shards(): slot_sum, slot_den = lax.psum((local_sum, local_den), 'tok')  18.4 us
    all_to_all x1, blocking collectives, shards(): lax.all_to_all(summed, 'exp', split_axis=2, concat_axis=1, tiled=True)  14.2 us
    dot_general x1, matrix products, shards(): jnp.einsum('std,dj->sjt', tokens, slot_params, preferred_element_type=jnp...  12.3 us
    dot_general x1, matrix products, shards(): jnp.einsum('sjt,std->sjd', dweight, tokens, preferred_element_type=jnp.fl...  11.7 us
  transfers between devices with their start and end apart: 2, of which 1 were waited for; matrix products, arithmetic and copies ran while one was open for 8% of the time, Pallas kernels for 0%

commit v1 on v0

--- a/solution.py
+++ b/solution.py
@@ -4,6 +4,11 @@
 from jax.sharding import PartitionSpec as P
 
 SLOTS_PER = 2
+
+
+def gather_and_add(x, mesh_axis):
+    terms = lax.all_gather(x, mesh_axis)
+    return jnp.sum(terms, axis=0)
 
 
 def shards(tokens, slot_params, w_in, w_out):
@@ -28,7 +33,7 @@
     ).astype(jnp.bfloat16)
     partial_out = jnp.einsum("sepf,efd->sepd", hidden, w_out, preferred_element_type=jnp.float32)
     partial_out = partial_out.reshape(seq_count, own_width, width)
-    summed = lax.psum(partial_out, "tok").astype(jnp.bfloat16)
+    summed = gather_and_add(partial_out, "tok").astype(jnp.bfloat16)
     slot_out = lax.all_to_all(summed, "exp", split_axis=2, concat_axis=1, tiled=True)
     comb_max = jnp.max(all_logits, axis=1)
     cexp = jnp.exp(all_logits - comb_max[:, None, :])

time: 547 us -> 426 us (0.78)
  blocking collectives: 383 us -> 41.5 us
  waiting for transfers between devices: 66.6 us -> 279 us
    psum x1 -> x0, blocking collectives: 327 us -> none  [shards(): summed = lax.psum(partial_out, 'tok').astype(jnp.bfloat16)]
    all_gather x0 -> x1, waiting for transfers between devices: none -> 175 us  [gather_and_add(): terms = lax.all_gather(x, mesh_axis)]
    all_gather x1, waiting for transfers between devices: 0.03 us -> 34.5 us  [shards(): all_logits = lax.all_gather(own_logits, 'exp', axis=1, tiled=True)]
    all_to_all x1 -> x0, blocking collectives: 14.2 us -> none  [shards(): lax.all_to_all(summed, 'exp', split_axis=2, concat_axis=1, tiled=True)]
    reshape x1 -> x0, local copies, waits for them, and re-layouts: 6.51 us -> none  [shards(): partial_out = partial_out.reshape(seq_count, own_width, width)]
    reduce_sum x0 -> x1, other arithmetic: none -> 6.16 us  [gather_and_add(): return jnp.sum(terms, axis=0)]
  transfers between devices with their start and end apart: 2 -> 4, of which waited for: 1 -> 3; matrix products, arithmetic and copies ran while one was open for 8% -> 5% of each run, Pallas kernels for 0% -> 0%
where the time goes in v1:
time: 426 us; the launch traced here: 425 us
  waiting for transfers between devices  279 us (65%)
  matrix products  51 us (12%)
  blocking collectives  41.5 us (10%)
  local copies, waits for them, and re-layouts  23.2 us (5%)
  other arithmetic  14.1 us (3%)
  between operations  13.2 us (3%)
    all_gather x1, waiting for transfers between devices, gather_and_add(): terms = lax.all_gather(x, mesh_axis)  175 us
    psum x1, waiting for transfers between devices, shards(): slot_sum, slot_den = lax.psum((local_sum, local_den), 'tok')  68.3 us
    all_gather x1, waiting for transfers between devices, shards(): all_logits = lax.all_gather(own_logits, 'exp', axis=1, tiled=True)  34.5 us
    pmax x1, blocking collectives, shards(): slot_peak = lax.pmax(local_max, 'tok')  23.4 us
    psum x1, blocking collectives, shards(): slot_sum, slot_den = lax.psum((local_sum, local_den), 'tok')  18.1 us
    dot_general x1, matrix products, shards(): jnp.einsum('std,dj->sjt', tokens, slot_params, preferred_element_type=jnp...  12.3 us
    dot_general x1, matrix products, shards(): jnp.einsum('sjt,std->sjd', dweight, tokens, preferred_element_type=jnp.fl...  11.7 us
    unnamed x8, local copies, waits for them, and re-layouts  10.8 us
  transfers between devices with their start and end apart: 4, of which 3 were waited for; matrix products, arithmetic and copies ran while one was open for 5% of the time, Pallas kernels for 0%

profile of v1, /device:TPU:0, one launch (start us, length us, event | category | flops | bytes accessed | tf_op | source)
XLA Modules:
  0.0 425.3 jit_solution(17810673530607237376)
XLA Ops:
  6.5 0.0 copy-start
  6.5 0.0 all-reduce.2.cloned.1.call-start
  6.5 0.8 copy-done
  7.4 12.3 %fusion.28 = (f32[12,32]{1,0:T(8,128)S(1)}, f32[12,32,1024]{2,1,0:T(8,128)S(1)}) fusion(bf16[12,1024,1024]{2,1,0:T(8,128)(2,1)} %param.4, bf16[1024,32]{0,1:T(8,128)(2,1)S(1)} %copy-done), kind=kOutput, calls=%fused_computation.28 | convolution fusion | flops 805699200 | bytes 26805760 | tf_op jit(solution)/shard_map/std,dj->sjt/dot_general | solution.py:16
  19.7 0.0 copy-start.2
  19.7 23.4 %pmax.7 = f32[12,32]{1,0:T(8,128)S(1)} all-reduce(f32[12,32]{1,0:T(8,128)S(1)} %get-tuple-element.5), channel_id=1, replica_groups=mesh['tok'=8,'exp'=4] {'tok'}, use_global_device_ids=true, to_apply=%region_3.0 | all-reduce | flops 384 | bytes 3072 | tf_op jit(solution)/shard_map/pmax | solution.py:19
  43.1 11.7 %fusion.23 = f32[12,32,1024]{2,1,0:T(8,128)} fusion(bf16[12,1024,1024]{2,1,0:T(8,128)(2,1)} %param.4, f32[12,32,1024]{2,1,0:T(8,128)S(1)} %get-tuple-element.6, f32[12,32]{1,0:T(8,128)S(1)} %pmax.7), kind=kOutput, calls=%fused_computation.24 | convolution fusion | flops 806092800 | bytes 28313088 | tf_op jit(solution)/shard_map/sjt,std->sjd/dot_general | solution.py:23
  54.7 0.0 all-reduce.2.cloned.1.call-update
  54.7 0.0 all-gather.5.cloned.1.call-start
  54.8 0.0 copy-done.2
  54.8 0.4 fusion.6
  55.2 18.1 %psum.15 = f32[12,32]{1,0:T(8,128)S(1)} all-reduce(f32[12,32]{1,0:T(8,128)S(1)} %fusion.6), channel_id=1, replica_groups=mesh['tok'=8,'exp'=4] {'tok'}, use_global_device_ids=true, to_apply=%region_6.0 | all-reduce | flops 384 | bytes 3072 | tf_op jit(solution)/shard_map/psum | solution.py:24
  73.3 68.3 %all-reduce.2.cloned.1.call-done = f32[12,32,1024]{2,1,0:T(8,128)} async-done(((f32[12,32,1024]{2,1,0:T(8,128)}), f32[12,32,1024]{2,1,0:T(8,128)}) %all-reduce.2.cloned.1.call-update) | async-done | bytes 1572880 | tf_op jit(solution)/shard_map/psum | solution.py:24
  141.6 1.6 divide_convert_fusion.2
  143.2 0.4 copy.28
  143.7 8.7 %fusion.20 = bf16[12,16,2,512]{3,0,2,1:T(8,128)(2,1)S(1)} fusion(bf16[12,16,2,1024]{3,0,2,1:T(8,128)(2,1)S(1)} %bitcast.48, bf16[16,1024,512]{2,1,0:T(8,128)(2,1)} %param.6), kind=kOutput, calls=%fused_computation.23 | convolution fusion | flops 404422656 | bytes 17956864 | tf_op jit(solution)/shard_map/sepd,edf->sepf/dot_general | solution.py:31
  152.4 8.7 %fusion.1 = f32[16,12,2,1024]{3,1,2,0:T(8,128)S(1)} fusion(bf16[12,16,2,512]{3,0,2,1:T(8,128)(2,1)S(1)} %fusion.20, bf16[16,512,1024]{2,1,0:T(8,128)(2,1)} %param.7), kind=kOutput, calls=%fused_computation.1 | convolution fusion | flops 402653184 | bytes 18743296 | tf_op jit(solution)/shard_map/sepf,efd->sepd/dot_general | solution.py:34
  161.2 2.1 copy.18
  163.3 0.0 all-gather.5.cloned.1.call-update
  163.3 0.2 all-gather.3.cloned.1.call-start
  163.5 0.5 all-gather.3.cloned.1.call-update
  164.0 175.2 %all-gather.5.cloned.1.call-done = f32[8,12,32,1024]{3,2,1,0:T(8,128)} async-done(((f32[1,12,32,1024]{3,2,1,0:T(8,128)}), f32[8,12,32,1024]{3,2,1,0:T(8,128)}) %all-gather.5.cloned.1.call-update) | async-done | bytes 12582928 | tf_op jit(solution)/shard_map/all_gather | solution.py:10
  339.3 6.2 %reduce_sum.29 = bf16[12,32,1024]{2,1,0:T(8,128)(2,1)S(1)} reduce(f32[8,12,32,1024]{3,2,1,0:T(8,128)} %all-gather.5.cloned.1.call-done, f32[]{:T(128)} %constant.1.clone.1), dimensions={0}, to_apply=%region_7.0 | reduce | flops 2752512 | bytes 13369348 | tf_op jit(solution)/shard_map/reduce_sum | solution.py:11
  345.4 4.7 %copy.21 = bf16[12,32,1024]{1,0,2:T(8,128)(2,1)} copy(bf16[12,32,1024]{2,1,0:T(8,128)(2,1)S(1)} %reduce_sum.29) | data formatting | bytes 1572864 | tf_op jit(solution)/shard_map/convert_element_type | solution.py:36
  350.1 5.8 %reshape.11 = bf16[4,2,49152]{2,1,0:T(2,128)(2,1)} reshape(bf16[1024,12,32]{2,1,0:T(8,128)(2,1)} %bitcast.45) | data formatting | bytes 1572864
  355.9 3.5 all-to-all-start
  359.4 34.5 %all-gather.3.cloned.1.call-done = f32[12,128,1024]{2,1,0:T(8,128)} async-done(((f32[12,32,1024]{2,1,0:T(8,128)}), f32[12,128,1024]{2,1,0:T(8,128)}) %all-gather.3.cloned.1.call-update) | async-done | bytes 6291472 | tf_op jit(solution)/shard_map/all_gather | solution.py:17
  393.8 6.0 %fusion.29 = f32[12,1024]{1,0:T(8,128)S(1)} fusion(f32[12,128,1024]{2,1,0:T(8,128)} %all-gather.3.cloned.1.call-done), kind=kOutput, calls=%fused_computation.29 | output fusion | flops 3145855 | bytes 6340608 | tf_op jit(solution)/shard_map/sub | solution.py:39
  399.8 0.0 all-to-all-done
  399.8 4.1 reshape.12
  404.0 5.1 %copy.29 = bf16[12,32,4,256]{3,2,1,0:T(4,128)(2,1)S(1)} copy(bf16[12,32,4,256]{1,0,3,2:T(8,128)(2,1)} %bitcast.46) | data formatting | bytes 1572864 | tf_op jit(solution)/shard_map/all_to_all | solution.py:37
  409.1 0.1 copy.23
  409.2 0.0 copy-start.1
  409.2 9.5 %convolution_convert_fusion = bf16[12,1024,256]{2,1,0:T(8,128)(2,1)} fusion(bf16[12,128,256]{2,1,0:T(8,128)(2,1)S(1)} %bitcast.50, f32[12,1024]{1,0:T(8,128)S(1)} %fusion.29, f32[12,128,1024]{2,1,0:T(8,128)} %all-gather.3.cloned.1.call-done), kind=kOutput, calls=%fused_computation.7 | convolution fusion | flops 813183104 | bytes 13418496 | tf_op jit(solution)/shard_map/sjt,sjd->std/dot_general | solution.py:41
  418.8 0.0 copy-done.1
Async XLA Ops:
  6.5 0.8 copy-start
  6.5 135.1 %all-reduce.2.cloned.1.call-start = ((), (), s32[]{:S(2)}) async-start(), calls=%async_computation.2 | async-start | bytes 3145728 | tf_op jit(solution)/shard_map/psum | solution.py:24
  19.7 35.1 %copy-start.2 = (f32[12,32,1024]{2,1,0:T(8,128)}, f32[12,32,1024]{2,1,0:T(8,128)S(1)}, u32[]{:S(2)}) copy-start(f32[12,32,1024]{2,1,0:T(8,128)S(1)} %get-tuple-element.6) | copy-start | bytes 4718596
  54.7 284.5 %all-gather.5.cloned.1.call-start = ((), (), s32[]{:S(2)}) async-start(), calls=%async_computation.3 | async-start | bytes 14155776 | tf_op jit(solution)/shard_map/all_gather | solution.py:10
  163.3 230.6 %all-gather.3.cloned.1.call-start = ((), (), s32[]{:S(2)}) async-start(), calls=%async_computation.1 | async-start | bytes 7864320 | tf_op jit(solution)/shard_map/all_gather | solution.py:17
  355.9 43.9 %all-to-all-start = ((bf16[4,2,49152]{2,1,0:T(2,128)(2,1)}), bf16[4,2,49152]{2,1,0:T(2,128)(2,1)S(1)}, u32[]{:S(2)}, u32[]{:S(2)}) async-start(bf16[4,2,49152]{2,1,0:T(2,128)(2,1)} %reshape.11), calls=%async_computation | async-start | bytes 1572864 | tf_op jit(solution)/shard_map/all_to_all | solution.py:37
  409.2 9.6 %copy-start.1 = (bf16[1024,32]{0,1:T(8,128)(2,1)S(1)}, bf16[1024,32]{0,1:T(8,128)(2,1)}, u32[]{:S(2)}) copy-start(bf16[1024,32]{0,1:T(8,128)(2,1)} %param.5) | copy-start | bytes 196612
Sparse Core Ops, SparseCore 0:
  54.9 86.7 all-reduce.1
  163.4 175.8 all-gather.4
  340.8 52.9 all-gather.2
